TPU v7x, 1024 devices: a whole 8x8x8 slice. The times are simulated.
1024 devices in a mesh: grp: 16 (over z, core), loc: 8 (over y), tp: 8 (over x).
Axes of the slice: x: 8, y: 8, z: 8, core: 2. Of those that a mesh axis runs over, the one named last changes fastest.
Arguments:
- tokens: bfloat16 [32768, 2048], P(('grp', 'tp')), may hold values from -6 to 6
- expert_ids: int32 [32768, 8], P(('grp', 'tp')), may hold values from 0 to 127, as said below
- router_weights: bfloat16 [32768, 8], P(('grp', 'tp')), may hold values from 0.19921875 to 1
- w_gate: bfloat16 [128, 2048, 768], P(('grp', 'loc')), may hold values from -0.125 to 0.125
- w_up: bfloat16 [128, 2048, 768], P(('grp', 'loc')), may hold values from -0.125 to 0.125
- w_down: bfloat16 [128, 768, 2048], P(('grp', 'loc'), None, 'tp'), may hold values from -0.21875 to 0.21875
Outputs:
- mixed: bfloat16 [32768, 2048], P(('grp', 'tp'), 'loc')
Inputs may be any that keep to these rules, and one draw needn't show every extreme that they name: `expert_ids`: each row names 8 different experts, two from each of 4 different groups, group g holding experts g * 8 to g * 8 + 7. Within each aligned block of 256 rows, no expert is named by more than 24 rows, and in every block some expert is named by exactly 24 rows.
All inputs are finite; a program needn't handle non-finite values.
Results may differ from a plain program's by a relative error of at most 0.0057.
Values may be sent and summed in bfloat16 or wider, within the bound.
A program may use at most 64 MiB of HBM per device.

v0:
```python
import jax
import jax.numpy as jnp
from jax import lax
from jax.sharding import PartitionSpec as P


def body(tokens, expert_ids, router_weights, w_gate, w_up, w_down):
    groups = lax.axis_size("grp")
    group_size = lax.axis_size("loc")
    own_local = lax.axis_index("loc")
    tok_rows, width_model = tokens.shape
    choices_per = expert_ids.shape[1]
    quantum = tok_rows // groups
    capacity = (2 * quantum * (4 + min(2, groups - 4)) + group_size - 1) // group_size
    slot_total = groups * capacity
    flat_expert = expert_ids.reshape(-1)
    flat_weight = router_weights.reshape(-1)
    token_row = jnp.arange(tok_rows * choices_per, dtype=jnp.int32) // choices_per
    targets = jnp.arange(groups, dtype=jnp.int32) * group_size + own_local
    hit_table = (flat_expert[:, None] == targets[None, :]).astype(jnp.int32)
    slot_rank = jnp.sum(jnp.cumsum(hit_table, axis=0) * hit_table, axis=1) - 1
    is_mine = jnp.sum(hit_table, axis=1) > 0
    slot_index = jnp.where(is_mine, flat_expert // group_size * capacity + slot_rank, slot_total)
    source_rows = (
        jnp.full((slot_total,), tok_rows, jnp.int32).at[slot_index].set(token_row, mode="drop")
    )
    outgoing = jnp.take(tokens, source_rows, axis=0, mode="fill", fill_value=0)
    arriving = lax.all_to_all(
        outgoing.reshape(groups, capacity, width_model),
        "grp",
        split_axis=0,
        concat_axis=0,
        tiled=True,
    )
    arriving = arriving.reshape(slot_total, width_model)
    gate_act = jnp.dot(arriving, w_gate[0], preferred_element_type=jnp.float32)
    upward = jnp.dot(arriving, w_up[0], preferred_element_type=jnp.float32)
    hidden = (jax.nn.silu(gate_act) * upward).astype(jnp.bfloat16)
    expert_out = jnp.dot(
        hidden,
        lax.all_gather(w_down[0], "tp", axis=1, tiled=True),
        preferred_element_type=jnp.float32,
    ).astype(jnp.bfloat16)
    mixing = (
        jnp.zeros((tok_rows, slot_total), jnp.bfloat16)
        .at[token_row, slot_index]
        .set(flat_weight, mode="drop")
    )
    returned = lax.all_to_all(
        expert_out.reshape(groups, capacity, width_model),
        "grp",
        split_axis=0,
        concat_axis=0,
        tiled=True,
    )
    local_sum = jnp.dot(
        mixing, returned.reshape(slot_total, width_model), preferred_element_type=jnp.float32
    )
    summed = lax.psum_scatter(local_sum, "loc", scatter_dimension=1, tiled=True)
    return summed.astype(jnp.bfloat16)


def solution(mesh):
    placed = (
        P(("grp", "tp"), None),
        P(("grp", "tp"), None),
        P(("grp", "tp"), None),
        P(("grp", "loc"), None, None),
        P(("grp", "loc"), None, None),
        P(("grp", "loc"), None, "tp"),
    )
    return jax.shard_map(
        body, mesh=mesh, in_specs=placed, out_specs=P(("grp", "tp"), "loc"), check_vma=False
    )
```

profile of v0, /device:TPU:1, one launch (start us, length us, event | category | flops | bytes accessed | tf_op | source)
XLA Modules:
  0.0 194.6 jit_solution(8811604657394029636)
XLA Ops:
  6.5 0.0 copy-start
  6.5 0.0 all-gather.3.cloned.1.call-start
  6.5 0.7 all-gather.3.cloned.1.call-update
  7.3 1.0 copy.7
  8.3 0.1 eq.29
  8.4 0.1 compare_convert_fusion.1
  8.5 4.5 %reduce-window.6 = s32[16,16,128]{2,1,0:T(8,128)S(1)} reduce-window(s32[16,16,128]{2,1,0:T(8,128)S(1)} %compare_convert_fusion.1, s32[]{:T(128)} %constant.57.clone.1), window={size=1x1x128 pad=0_0x0_0x127_0}, to_apply=%region_1.2 | reduce-window | flops 4161536 | bytes 262148 | tf_op jit(solution)/shard_map/reduce-window
  13.1 0.4 slice_reduce_fusion
  13.5 0.2 reduce-window.9
  13.7 0.1 broadcast_add_fusion
  13.8 0.1 eq.25
  13.9 0.1 reshape.200
  14.0 0.1 fusion.19
  14.2 0.1 compare_select_fusion.1
  14.3 8.0 %scatter_custom_fusion = s32[384]{0:T(512)S(1)} fusion(s32[2048]{0:T(1024)S(1)} %bitcast.42, s32[2048]{0:T(1024)S(1)} %add_select_fusion, s32[]{:T(128)} %constant.60.clone.1), kind=kCustom, calls=%fused_computation.51 | custom fusion | bytes 1540 | tf_op jit(solution)/shard_map/scatter | solution.py:25
  22.3 0.1 broadcast_in_dim.31
  22.4 6.4 %gather_fusion = bf16[384,2048]{1,0:T(8,128)(2,1)} fusion(bf16[256,2048]{1,0:T(8,128)(2,1)} %param.6, s32[1024]{0:T(1024)S(1)} %pad_clamp_fusion), kind=kCustom, calls=%fused_computation | custom fusion | bytes 3147264 | tf_op jit(solution)/shard_map/jit(_take)/gather | solution.py:27
  28.8 1.6 broadcast_select_fusion
  30.4 0.0 copy-start.5
  30.4 57.9 %all_to_all.10 = bf16[16,24,2048]{2,1,0:T(8,128)(2,1)S(1)} all-to-all(bf16[16,24,2048]{2,1,0:T(8,128)(2,1)S(1)} %broadcast_select_fusion), channel_id=1, replica_groups=mesh['grp'=16,'loc'=8,'tp'=8] {'grp'}, dimensions={0} | all-to-all | bytes 3145728 | tf_op jit(solution)/shard_map/all_to_all | solution.py:28
  88.4 0.0 copy-start.1
  88.4 1.2 copy-done.1
  89.6 0.0 copy-done.5
  89.6 2.5 %fusion.4 = f32[384,768]{1,0:T(8,128)} fusion(bf16[384,2048]{1,0:T(8,128)(2,1)S(1)} %bitcast.39, bf16[1,2048,768]{2,1,0:T(8,128)(2,1)S(1)} %copy-done.5), kind=kOutput, calls=%fused_computation.7 | convolution fusion | flops 1207959552 | bytes 5898240 | tf_op jit(solution)/shard_map/dot_general | solution.py:36
  92.0 0.0 all-gather.3.cloned.1.call-done
  92.0 0.0 copy-done
  92.0 6.9 %fusion.6 = bf16[384,2048]{1,0:T(8,128)(2,1)} fusion(bf16[1,768,2048]{2,1,0:T(8,128)(2,1)} %all-gather.3.cloned.1.call-done, bf16[384,2048]{1,0:T(8,128)(2,1)} %bitcast.40, bf16[1,2048,768]{2,1,0:T(8,128)(2,1)S(1)} %copy-done, f32[384,768]{1,0:T(8,128)} %fusion.4), kind=kOutput, calls=%fused_computation.9 | convolution fusion | flops 2418475008 | bytes 10616832 | tf_op jit(solution)/shard_map/dot_general | solution.py:39
  98.9 0.0 copy-start.2
  98.9 0.0 copy-start.4
  98.9 0.0 copy-start.3
  98.9 4.4 %all-to-all-start.1 = ((bf16[16,24,2048]{2,1,0:T(8,128)(2,1)}), bf16[16,24,2048]{2,1,0:T(8,128)(2,1)}, u32[]{:S(2)}, u32[]{:S(2)}) async-start(bf16[16,24,2048]{2,1,0:T(8,128)(2,1)} %bitcast.38), calls=%async_computation.1 | async-start | bytes 3145728 | tf_op jit(solution)/shard_map/all_to_all | solution.py:49
  103.4 0.2 reduce-scatter.2.cloned.1.call-start
  103.6 0.0 copy-done.2
  103.6 0.1 copy.10
  103.7 0.1 reshape.228
  103.9 0.0 copy-done.4
  103.9 0.1 multiply_reduce_fusion
  104.0 0.0 copy-done.3
  104.0 0.1 and_reduce_fusion
  104.1 14.7 %scatter_custom_fusion.1 = bf16[98304]{0:T(1024)(128)(2,1)S(1)} fusion(s32[2048]{0:T(1024)S(1)} %broadcast_select_fusion.1, bf16[2048]{0:T(1024)(128)(2,1)S(1)} %reshape.228, bf16[]{:T(256)} %constant.54.clone.1), kind=kCustom, calls=%fused_computation.21 | custom fusion | bytes 196610
  118.8 0.1 reshape.209
  118.9 21.5 %all-to-all-done.1 = bf16[16,24,2048]{2,1,0:T(8,128)(2,1)} async-done(((bf16[16,24,2048]{2,1,0:T(8,128)(2,1)}), bf16[16,24,2048]{2,1,0:T(8,128)(2,1)}, u32[]{:S(2)}, u32[]{:S(2)}) %all-to-all-start.1) | async-done | bytes 1572896 | tf_op jit(solution)/shard_map/all_to_all | solution.py:49
  140.4 3.5 %fusion.28 = f32[256,2048]{1,0:T(8,128)} fusion(bf16[256,384]{1,0:T(8,128)(2,1)S(1)} %reshape.209, bf16[384,2048]{1,0:T(8,128)(2,1)} %bitcast.9), kind=kOutput, calls=%fused_computation.55 | convolution fusion | flops 402653184 | bytes 3866624 | tf_op jit(solution)/shard_map/dot_general | solution.py:56
  143.8 0.0 reduce-scatter.2.cloned.1.call-update
  143.9 42.3 %reduce-scatter.2.cloned.1.call-done = f32[256,256]{1,0:T(8,128)} async-done(((f32[256,2048]{1,0:T(8,128)}), f32[256,256]{1,0:T(8,128)}) %reduce-scatter.2.cloned.1.call-update) | async-done | bytes 262160 | tf_op jit(solution)/shard_map/reduce_scatter | solution.py:59
  186.1 1.6 convert_element_type.20
  (8 shorter events, 0.0 us)
Async XLA Ops:
  6.5 85.5 %copy-start = (bf16[1,2048,768]{2,1,0:T(8,128)(2,1)S(1)}, bf16[1,2048,768]{2,1,0:T(8,128)(2,1)}, u32[]{:S(2)}) copy-start(bf16[1,2048,768]{2,1,0:T(8,128)(2,1)} %param.10) | copy-start | bytes 9437188
  6.5 85.5 %all-gather.3.cloned.1.call-start = ((), (), s32[]{:S(2)}) async-start(), calls=%async_computation.4 | async-start | bytes 3538944 | tf_op jit(solution)/shard_map/all_gather | solution.py:41
  30.4 59.1 %copy-start.5 = (bf16[1,2048,768]{2,1,0:T(8,128)(2,1)S(1)}, bf16[1,2048,768]{2,1,0:T(8,128)(2,1)}, u32[]{:S(2)}) copy-start(bf16[1,2048,768]{2,1,0:T(8,128)(2,1)} %param.9) | copy-start | bytes 9437188
  88.4 1.2 copy-start.1
  98.9 4.7 %copy-start.2 = (bf16[256,8]{0,1:T(8,128)(2,1)S(1)}, bf16[256,8]{0,1:T(8,128)(2,1)}, u32[]{:S(2)}) copy-start(bf16[256,8]{0,1:T(8,128)(2,1)} %param.8) | copy-start | bytes 12292
  98.9 4.9 %copy-start.4 = (s32[2]{0:T(128)S(1)}, s32[2]{0:T(128)}, u32[]{:S(2)}) copy-start(s32[2]{0:T(128)} %constant.71) | copy-start | bytes 28
  98.9 5.0 %copy-start.3 = (s32[2]{0:T(128)S(1)}, s32[2]{0:T(128)}, u32[]{:S(2)}) copy-start(s32[2]{0:T(128)} %constant.74) | copy-start | bytes 28
  98.9 41.4 %all-to-all-start.1 = ((bf16[16,24,2048]{2,1,0:T(8,128)(2,1)}), bf16[16,24,2048]{2,1,0:T(8,128)(2,1)}, u32[]{:S(2)}, u32[]{:S(2)}) async-start(bf16[16,24,2048]{2,1,0:T(8,128)(2,1)} %bitcast.38), calls=%async_computation.1 | async-start | bytes 3145728 | tf_op jit(solution)/shard_map/all_to_all | solution.py:49
  103.4 82.8 %reduce-scatter.2.cloned.1.call-start = ((), (), s32[]{:S(2)}) async-start(), calls=%async_computation.3 | async-start | bytes 2359296 | tf_op jit(solution)/shard_map/reduce_scatter | solution.py:59
Sparse Core Ops, SparseCore 0:
  9.9 68.7 all-gather.2
  144.0 42.1 reduce-scatter.1
where the time goes:
time: 198 us; the launch traced here: 195 us
  waiting for transfers between devices  64.5 us (33%)
  blocking collectives  57.9 us (29%)
  local copies, waits for them, and re-layouts  32.6 us (16%)
  between operations  13.6 us (7%)
  matrix products  12.8 us (6%)
  other arithmetic  8.53 us (4%)
  starting transfers between devices  4.65 us (2%)
    all_to_all x1, blocking collectives, body(): lax.all_to_all(outgoing.reshape(groups, capacity, width_model), 'grp', sp...  57.9 us
    reduce_scatter x1, waiting for transfers between devices, body(): summed = lax.psum_scatter(local_sum, 'loc', scatter_dimension=1, tiled=True)  42.3 us
    all_to_all x1, waiting for transfers between devices, body(): lax.all_to_all(expert_out.reshape(groups, capacity, width_model), 'grp',...  21.5 us
    unnamed x15, local copies, waits for them, and re-layouts  17 us
    scatter x1, local copies, waits for them, and re-layouts, body(): jnp.full((slot_total,), tok_rows, jnp.int32).at[slot_index]  8.04 us
    dot_general x1, matrix products, body(): jnp.dot(hidden, lax.all_gather(w_down[0], 'tp', axis=1, tiled=True), pref...  6.91 us
    gather x1, local copies, waits for them, and re-layouts, body(): outgoing = jnp.take(tokens, source_rows, axis=0, mode='fill', fill_value=0)  6.41 us
    another operation x3, other arithmetic  4.82 us
  transfers between devices with their start and end apart: 3, of which 2 were waited for; matrix products, arithmetic and copies ran while one was open for 21% of the time, Pallas kernels for 0%

commit v1 on v0

v1 whole, which is shorter than its diff:
```python
import jax
import jax.numpy as jnp
from jax import lax
from jax.experimental import pallas as pl
from jax.experimental.pallas import tpu as pltpu
from jax.sharding import PartitionSpec as P

MESH = pl.DeviceIdType.MESH
F32 = jnp.float32
BF16 = jnp.bfloat16
RING = 8
CAP = 24
ROWS = 2 * CAP
POS = {0: 0, 1: 1, 7: 2, 2: 3, 6: 4, 3: 5, 5: 6, 4: 7}
OFFSETS = (6, 2, 0, 7, 1)
IN_SLICES = (0, 4, 1, 5, 7, 3, 2, 6)
BACK = ((1, 1, 3), (5, 1, 6), (7, 7, 4), (3, 7, 7), (2, 2, 0), (6, 6, 1))
BACK_SELF = ((0, 2), (4, 5))


def kernel(meta, tok, wg, wu, wd, o_ref,
           xa, xb, sel, selw, xs, xr, wgs, wus, wds, hid, ob, yr, pk, pp, sp, sm, rp, rm, fs, fr, tri,
           lsem, wsem, zs, zr, cs, cr, ds_s, ds_r, xs_s, xs_r, bs, br, ps, pr, rps, rpr, rms, rmr, fsem):
    g = lax.axis_index("grp")
    l = lax.axis_index("loc")
    t = lax.axis_index("tp")
    z = g // 2
    c = g % 2
    other = 1 - c
    tok_rows = tok.shape[0]
    width = o_ref.shape[1]
    ff = wds.shape[1]
    half_ff = ff // 2

    def z_to(step):
        return {"grp": ((z + step) % RING) * 2 + c}

    def y_to(step):
        return {"loc": (l + step) % RING}

    def x_to(step):
        return {"tp": (t + step) % RING}

    partner = {"grp": z * 2 + other}

    def remote(src, dst, send, recv, dev):
        return pltpu.make_async_remote_copy(
            src_ref=src, dst_ref=dst, send_sem=send, recv_sem=recv, device_id=dev, device_id_type=MESH
        )

    started = []

    def go(copy):
        copy.start()
        started.append(copy)

    def cols(off):
        return pl.ds(pl.multiple_of(((l + off) % RING) * width, width), width)

    load_a = pltpu.make_async_copy(tok.at[:, cols(0)], xa.at[0, c, pl.ds(0, tok_rows), :], lsem.at[0])
    load_b = pltpu.make_async_copy(tok.at[:, cols(4)], xb.at[0, c], lsem.at[1])
    load_m = pltpu.make_async_copy(meta, xa.at[0, c, pl.ds(tok_rows, 16), :], lsem.at[2])
    load_d = pltpu.make_async_copy(wd.at[0], wds.at[0], lsem.at[3])
    for copy in (load_a, load_m, load_b, load_d):
        copy.start()
    weight_loads = []
    for i, off in enumerate(IN_SLICES):
        for j, (src, dst) in enumerate(((wg, wgs), (wu, wus))):
            copy = pltpu.make_async_copy(src.at[0, cols(off), :], dst.at[pl.ds(i * width, width), :], wsem.at[j, i])
            copy.start()
            weight_loads.append(copy)

    barrier = pltpu.get_barrier_semaphore()
    peers = [z_to(1), z_to(7), partner, y_to(1), y_to(7), y_to(2), y_to(6), y_to(4), x_to(1), x_to(7)]
    for peer in peers:
        pl.semaphore_signal(barrier, inc=1, device_id=peer, device_id_type=MESH)
    pl.semaphore_wait(barrier, len(peers))

    halves = (xa, xb)

    def z_copy(dz, h, step):
        to = (dz - step) % RING
        return remote(
            halves[h].at[POS[dz % RING], c], halves[h].at[POS[to], c],
            zs.at[h, POS[to]], zr.at[h, POS[to]], z_to(step),
        )

    def c_copy(dz, h):
        p = POS[dz % RING]
        return remote(halves[h].at[p, c], halves[h].at[p, c], cs.at[h, p], cr.at[h, p], partner)

    def d_copy(rel, h, step):
        to = (rel - step) % RING
        rows = pl.ds(h * half_ff, half_ff)
        return remote(
            wds.at[rel % RING, rows, :], wds.at[to, rows, :], ds_s.at[h, to], ds_r.at[h, to], x_to(step)
        )

    def z_event(step, h):
        dirs = []
        if step < 4 or h == 0:
            dirs.append((1, -step))
        if step < 4 or h == 1:
            dirs.append((-1, step))
        for way, dz in dirs:
            if step > 0:
                z_copy(dz + way, h, way).wait_recv()
            if step < 3 or (step == 3 and (h == 0) == (way == 1)):
                go(z_copy(dz, h, way))
            if step > 0 or way == 1:
                go(c_copy(dz, h))

    def x_event(step, h):
        dirs = []
        if step < 4 or h == 0:
            dirs.append((1, -step))
        if step < 4 or h == 1:
            dirs.append((-1, step))
        for way, rel in dirs:
            if step > 0:
                d_copy(rel + way, h, way).wait_recv()
            if step < 3 or (step == 3 and (h == 0) == (way == 1)):
                go(d_copy(rel, h, way))

    row_ids = lax.broadcasted_iota(jnp.int32, (8, 1), 0)
    offs = jnp.zeros((8, 1), jnp.int32)
    for j, off in enumerate(OFFSETS):
        offs = jnp.where(row_ids == j, off, offs)
    locs = l + offs
    locs = jnp.where(locs >= RING, locs - RING, locs)
    targets = jnp.where(row_ids < len(OFFSETS), g * RING + locs, -1).astype(F32)
    slot_ids = lax.broadcasted_iota(jnp.int32, (ROWS, tok_rows), 0).astype(F32)

    OUT = ((1, 4 * ROWS, 0, 4, 2), (7, 3 * ROWS, 2, 2, 2), (6, 0, 4, 6, 1), (2, ROWS, 5, 7, 1))

    def y_copy(p, k):
        off, _, src, dst, n = OUT[k]
        return remote(
            xs.at[p, :, pl.ds(src * width, n * width)], xr.at[p, :, pl.ds(dst * width, n * width)],
            xs_s.at[k, p], xs_r.at[k, p], y_to(off),
        )

    def select(dz):
        p = POS[dz]
        for h in range(2):
            c_copy(dz, h).wait_recv()
        hits = []
        weights = []
        for core in range(2):
            info = xa[p, core, pl.ds(tok_rows, 16), :].astype(F32)
            hit = jnp.zeros((8, tok_rows), F32)
            weight = jnp.zeros((8, tok_rows), F32)
            for k in range(8):
                same = info[k:k + 1, :] == targets
                hit = jnp.where(same, 1.0, hit)
                weight = jnp.where(same, info[8 + k:9 + k, :], weight)
            hits.append(hit)
            weights.append(weight)
        both = jnp.concatenate(hits, axis=0)
        rank = jnp.dot(both.astype(BF16), tri[...], preferred_element_type=F32)
        for core in range(2):
            place = jnp.where(hits[core] > 0.5, rank[8 * core:8 * core + 8, :] + float(core * CAP), -1.0)
            for j in range(len(OFFSETS)):
                same = slot_ids == place[j:j + 1, :]
                where = (p, pl.ds(j * ROWS, ROWS), pl.ds(core * tok_rows, tok_rows))
                sel[where] = jnp.where(same, 1.0, 0.0).astype(BF16)
                selw[where] = jnp.where(same, weights[core][j:j + 1, :], 0.0).astype(BF16)
        first = sel[p, :, pl.ds(0, tok_rows)]
        second = sel[p, :, pl.ds(tok_rows, tok_rows)]
        x0 = (
            jnp.dot(first, xa[p, 0, pl.ds(0, tok_rows), :], preferred_element_type=F32)
            + jnp.dot(second, xa[p, 1, pl.ds(0, tok_rows), :], preferred_element_type=F32)
        ).astype(BF16)
        x1 = (
            jnp.dot(first[2 * ROWS:, :], xb[p, 0], preferred_element_type=F32)
            + jnp.dot(second[2 * ROWS:, :], xb[p, 1], preferred_element_type=F32)
        ).astype(BF16)
        for k, (_, row, src, _, n) in enumerate(OUT):
            xs[p, :, pl.ds(src * width, width)] = x0[row:row + ROWS, :]
            if n == 2:
                xs[p, :, pl.ds((src + 1) * width, width)] = x1[row - 2 * ROWS:row - ROWS, :]
            go(y_copy(p, k))
        xr[p, :, pl.ds(0, width)] = x0[2 * ROWS:3 * ROWS, :]
        xr[p, :, pl.ds(width, width)] = x1[:ROWS, :]

    def gate_up(first, count):
        for p in range(first, first + count):
            for k in range(4):
                y_copy(p, k).wait_recv()
        x = xr[pl.ds(first, count)].reshape(count * ROWS, RING * width)
        rows = pl.ds(first * ROWS, count * ROWS)
        for n in range(ff // 256):
            part = pl.ds(n * 256, 256)
            gate = jnp.dot(x, wgs[:, part], preferred_element_type=F32)
            up = jnp.dot(x, wus[:, part], preferred_element_type=F32)
            hid[rows, part] = (gate / (1.0 + jnp.exp(-gate)) * up).astype(BF16)

    load_a.wait()
    load_m.wait()
    z_event(0, 0)
    load_b.wait()
    z_event(0, 1)
    load_d.wait()
    x_event(0, 0)
    x_event(0, 1)
    tri[...] = jnp.where(
        lax.broadcasted_iota(jnp.int32, (tok_rows, tok_rows), 0) < lax.broadcasted_iota(jnp.int32, (tok_rows, tok_rows), 1),
        1.0, 0.0,
    ).astype(BF16)
    select(0)
    z_event(1, 0)
    x_event(1, 0)
    z_event(1, 1)
    select(1)
    select(7)
    x_event(1, 1)
    z_event(2, 0)
    z_event(2, 1)
    x_event(2, 0)
    select(2)
    select(6)
    for copy in weight_loads:
        copy.wait()
    z_event(3, 0)
    gate_up(0, 3)
    x_event(2, 1)
    z_event(3, 1)
    select(3)
    select(5)
    z_event(4, 0)
    z_event(4, 1)
    x_event(3, 0)
    select(4)
    gate_up(3, 2)
    x_event(3, 1)
    gate_up(5, 3)
    x_event(4, 0)
    x_event(4, 1)

    def b_copy(p, k):
        _, off, window = BACK[k]
        return remote(ob.at[p, k], yr.at[p, window], bs.at[k, p], br.at[k, p], y_to(off))

    def down(first, count):
        h = hid[pl.ds(first * ROWS, count * ROWS), :]
        for k, (off, _, _) in enumerate(BACK):
            y = jnp.dot(h, wds[(l + off + RING - t) % RING], preferred_element_type=F32).astype(BF16)
            for i in range(count):
                ob[first + i, k] = y[i * ROWS:(i + 1) * ROWS, :]
        for p in reversed(range(first, first + count)):
            for k in range(len(BACK)):
                go(b_copy(p, k))
        for off, window in BACK_SELF:
            y = jnp.dot(h, wds[(l + off + RING - t) % RING], preferred_element_type=F32).astype(BF16)
            for i in range(count):
                yr[first + i, window] = y[i * ROWS:(i + 1) * ROWS, :]

    down(5, 3)
    down(3, 2)
    down(0, 3)

    def p_copy(dz):
        p = POS[dz]
        return remote(pk.at[p, other], pp.at[p], ps.at[p], pr.at[p], partner)

    def mix(dz):
        p = POS[dz]
        for k in range(len(BACK)):
            b_copy(p, k).wait_recv()
        for h, (row, lo, n) in enumerate(((0, 0, 5), (2 * ROWS, 5, 3))):
            part = lax.dot_general(
                selw[p, pl.ds(row, n * ROWS), :], yr[p, pl.ds(lo, n)].reshape(n * ROWS, width),
                (((0,), (0,)), ((), ())), preferred_element_type=F32,
            ).astype(BF16)
            pk[p, 0, h] = part[:tok_rows, :]
            pk[p, 1, h] = part[tok_rows:, :]
        go(p_copy(dz))

    def chip_sum(dz, h):
        p = POS[dz]
        return pk[p, c, h].astype(F32) + pp[p, h].astype(F32)

    def r_copy(way, s, h):
        src, dst, send, recv = (sp, rp, rps, rpr) if way == 1 else (sm, rm, rms, rmr)
        return remote(src.at[s - 1, h], dst.at[s - 1, h], send.at[s - 1, h], recv.at[s - 1, h], z_to(way))

    def ring(way, s, h):
        value = chip_sum(s if way == 1 else RING - s, h)
        if s < 3 or (s == 3 and (h == 0) == (way == 1)):
            r_copy(way, s + 1, h).wait_recv()
            value += (rp if way == 1 else rm)[s, h].astype(F32)
        (sp if way == 1 else sm)[s - 1, h] = value.astype(BF16)
        go(r_copy(way, s, h))

    mix(4)
    mix(3)
    p_copy(4).wait_recv()
    ring(1, 4, 0)
    ring(-1, 4, 1)
    mix(5)
    p_copy(3).wait_recv()
    p_copy(5).wait_recv()
    ring(1, 3, 1)
    ring(-1, 3, 0)
    mix(2)
    mix(6)
    ring(1, 3, 0)
    ring(-1, 3, 1)
    p_copy(2).wait_recv()
    p_copy(6).wait_recv()
    mix(1)
    mix(7)
    ring(1, 2, 1)
    ring(-1, 2, 1)
    ring(1, 2, 0)
    ring(-1, 2, 0)
    mix(0)
    p_copy(1).wait_recv()
    p_copy(7).wait_recv()
    ring(1, 1, 1)
    ring(-1, 1, 1)
    ring(1, 1, 0)
    ring(-1, 1, 0)
    p_copy(0).wait_recv()

    def total(h):
        value = chip_sum(0, h)
        for way, buf in ((1, rp), (-1, rm)):
            r_copy(way, 1, h).wait_recv()
            value += buf[0, h].astype(F32)
        return value

    last = remote(fs, fr, fsem.at[0], fsem.at[1], y_to(4))
    fs[...] = total(1).astype(BF16)
    go(last)
    own = total(0)
    last.wait_recv()
    o_ref[...] = (own + fr[...].astype(F32)).astype(BF16)
    for copy in started:
        copy.wait_send()


def body(tokens, expert_ids, router_weights, w_gate, w_up, w_down):
    rows, width_model = tokens.shape
    ff = w_gate.shape[2]
    width = width_model // RING
    meta = jnp.concatenate([expert_ids.T.astype(BF16), router_weights.T], axis=0)
    dma = pltpu.SemaphoreType.DMA
    anywhere = pl.BlockSpec(memory_space=pl.ANY)
    return pl.pallas_call(
        kernel,
        out_shape=jax.ShapeDtypeStruct((rows, width), BF16),
        in_specs=[anywhere] * 5,
        out_specs=pl.BlockSpec(memory_space=pltpu.VMEM),
        scratch_shapes=[
            pltpu.VMEM((8, 2, rows + 16, width), BF16),
            pltpu.VMEM((8, 2, rows, width), BF16),
            pltpu.VMEM((8, 5 * ROWS, 2 * rows), BF16),
            pltpu.VMEM((8, 5 * ROWS, 2 * rows), BF16),
            pltpu.VMEM((8, ROWS, 6 * width), BF16),
            pltpu.VMEM((8, ROWS, 8 * width), BF16),
            pltpu.VMEM((width_model, ff), BF16),
            pltpu.VMEM((width_model, ff), BF16),
            pltpu.VMEM((8, ff, width), BF16),
            pltpu.VMEM((8 * ROWS, ff), BF16),
            pltpu.VMEM((8, 6, ROWS, width), BF16),
            pltpu.VMEM((8, 8, ROWS, width), BF16),
            pltpu.VMEM((8, 2, 2, rows, width), BF16),
            pltpu.VMEM((8, 2, rows, width), BF16),
            pltpu.VMEM((4, 2, rows, width), BF16),
            pltpu.VMEM((4, 2, rows, width), BF16),
            pltpu.VMEM((4, 2, rows, width), BF16),
            pltpu.VMEM((4, 2, rows, width), BF16),
            pltpu.VMEM((rows, width), BF16),
            pltpu.VMEM((rows, width), BF16),
            pltpu.VMEM((rows, rows), BF16),
            dma((4,)), dma((2, 8)),
            dma((2, 8)), dma((2, 8)), dma((2, 8)), dma((2, 8)),
            dma((2, 8)), dma((2, 8)), dma((4, 8)), dma((4, 8)),
            dma((6, 8)), dma((6, 8)), dma((8,)), dma((8,)),
            dma((4, 2)), dma((4, 2)), dma((4, 2)), dma((4, 2)), dma((2,)),
        ],
        compiler_params=pltpu.CompilerParams(
            collective_id=0, has_side_effects=True, vmem_limit_bytes=60 * 1024 * 1024
        ),
    )(meta, tokens, w_gate, w_up, w_down)


def solution(mesh):
    placed = (
        P(("grp", "tp"), None),
        P(("grp", "tp"), None),
        P(("grp", "tp"), None),
        P(("grp", "loc"), None, None),
        P(("grp", "loc"), None, None),
        P(("grp", "loc"), None, "tp"),
    )
    return jax.shard_map(
        body, mesh=mesh, in_specs=placed, out_specs=P(("grp", "tp"), "loc"), check_vma=False
    )
```

time: 198 us -> 102 us (0.52)
  the two profiles are of different devices: /device:TPU:1 before, /device:TPU:2 now
where the time goes in v1:
time: 102 us
  Pallas kernels  98.1 us (96%)
  other arithmetic  1.98 us (2%)
  local copies, waits for them, and re-layouts  1.57 us (2%)
    pallas_call x1, Pallas kernels, body(): pl.pallas_call(kernel, out_shape=jax.ShapeDtypeStruct((rows, width), BF16...  98.1 us

profile of v1, /device:TPU:2, one launch (start us, length us, event | category | flops | bytes accessed | tf_op | source)
XLA Modules:
  0.0 101.7 jit_solution(18107192319274663484)
XLA Ops:
  0.0 0.7 convert_bitcast_fusion
  0.7 1.3 %pad_maximum_fusion.meta = bf16[16,256]{1,0:T(8,128)(2,1)} fusion(bf16[8,256]{1,0:T(8,128)(2,1)} %bitcast.3, bf16[8,256]{1,0:T(8,128)(2,1)S(1)} %convert_bitcast_fusion), kind=kLoop, calls=%fused_computation | loop fusion | flops 16384 | bytes 16384 | tf_op jit(solution)/shard_map/concatenate | solution.py:347
  2.0 98.1 %shard_map.64 = bf16[256,256]{1,0:T(8,128)(2,1)} custom-call(bf16[16,256]{1,0:T(8,128)(2,1)} %pad_maximum_fusion.meta, bf16[256,2048]{1,0:T(8,128)(2,1)} %tok.1, bf16[1,2048,768]{2,1,0:T(8,128)(2,1)} %wg.1, bf16[1,2048,768]{2,1,0:T(8,128)(2,1)} %wu.1, bf16[1,768,256]{2,1,0:T(8,128)(2,1)} %wd.1), custom_call_target="tpu_custom_call" | custom-call | tf_op jit(solution)/shard_map/pallas_call | solution.py:350
  100.1 1.6 %copy.8 = bf16[256,256]{1,0:T(8,128)(2,1)} copy(bf16[256,256]{1,0:T(8,128)(2,1)} %shard_map.64) | data formatting | bytes 262144

commit v2 on v1

v2 whole, which is shorter than its diff:
```python
import jax
import jax.numpy as jnp
from jax import lax
from jax.experimental import pallas as pl
from jax.experimental.pallas import tpu as pltpu
from jax.sharding import PartitionSpec as P

MESH = pl.DeviceIdType.MESH
F32 = jnp.float32
BF16 = jnp.bfloat16
RING = 8
CAP = 24
ROWS = 2 * CAP
Z_PARTS = 2
X_PARTS = 2
R_PARTS = 2
POS = {0: 0, 1: 1, 7: 2, 2: 3, 6: 4, 3: 5, 5: 6, 4: 7}
OFFSETS = (6, 2, 0, 7, 1)
IN_SLICES = (0, 4, 1, 5, 7, 3, 2, 6)
BACK = ((1, 1, 3), (5, 1, 6), (7, 7, 4), (3, 7, 7), (2, 2, 0), (6, 6, 1))
BACK_SELF = ((0, 2), (4, 5))


def kernel(ids, gains, tok, wg, wu, wd, o_ref,
           xa, xb, sel, selw, xs, xr, wgs, wus, wds, hid, ob, yr, pk, pp, sp, sm, rp, rm, fs, fr, fa, tri, ids_v, gains_v,
           lsem, wsem, zs, zr, cs, cr, ds_s, ds_r, xs_s, xs_r, bs, br, ps, pr, rps, rpr, rms, rmr, fsem):
    g = lax.axis_index("grp")
    l = lax.axis_index("loc")
    t = lax.axis_index("tp")
    z = g // 2
    c = g % 2
    other = 1 - c
    tok_rows = tok.shape[0]
    width = o_ref.shape[1]
    ff = wds.shape[1]
    piece_ff = ff // (2 * X_PARTS)
    piece = tok_rows // R_PARTS

    def z_to(step):
        return {"grp": ((z + step) % RING) * 2 + c}

    def y_to(step):
        return {"loc": (l + step) % RING}

    def x_to(step):
        return {"tp": (t + step) % RING}

    partner = {"grp": z * 2 + other}

    def remote(src, dst, send, recv, dev):
        return pltpu.make_async_remote_copy(
            src_ref=src, dst_ref=dst, send_sem=send, recv_sem=recv, device_id=dev, device_id_type=MESH
        )

    started = []

    def go(copy):
        copy.start()
        started.append(copy)

    def cols(off):
        return pl.ds(pl.multiple_of(((l + off) % RING) * width, width), width)

    load_a = pltpu.make_async_copy(tok.at[:, cols(0)], xa.at[0, c, pl.ds(0, tok_rows), :], lsem.at[0])
    load_b = pltpu.make_async_copy(tok.at[:, cols(4)], xb.at[0, c], lsem.at[1])
    load_i = pltpu.make_async_copy(ids, ids_v, lsem.at[2])
    load_g = pltpu.make_async_copy(gains, gains_v, lsem.at[4])
    load_d = pltpu.make_async_copy(wd.at[0], wds.at[0], lsem.at[3])
    for copy in (load_d, load_b, load_i, load_g, load_a):
        copy.start()
    weight_loads = []
    for i, off in enumerate(IN_SLICES):
        for j, (src, dst) in enumerate(((wg, wgs), (wu, wus))):
            copy = pltpu.make_async_copy(src.at[0, cols(off), :], dst.at[pl.ds(i * width, width), :], wsem.at[j, i])
            weight_loads.append(copy)

    barrier = pltpu.get_barrier_semaphore()
    peers = [z_to(1), z_to(7), partner, y_to(1), y_to(7), y_to(2), y_to(6), x_to(1), x_to(7)]
    for peer in peers:
        pl.semaphore_signal(barrier, inc=1, device_id=peer, device_id_type=MESH)
    pl.semaphore_wait(barrier, len(peers))

    halves = (xa, xb)

    def z_copy(dz, h, r, step):
        to = (dz - step) % RING
        size = tok_rows // Z_PARTS
        extra = 16 if h == 0 and r == Z_PARTS - 1 else 0
        rows = pl.ds(r * size, size + extra)
        return remote(
            halves[h].at[POS[dz % RING], c, rows, :], halves[h].at[POS[to], c, rows, :],
            zs.at[h, r, POS[to]], zr.at[h, r, POS[to]], z_to(step),
        )

    def c_copy(dz, h):
        p = POS[dz % RING]
        return remote(halves[h].at[p, c], halves[h].at[p, c], cs.at[h, p], cr.at[h, p], partner)

    def d_copy(rel, q, step):
        to = (rel - step) % RING
        rows = pl.ds(q * piece_ff, piece_ff)
        return remote(
            wds.at[rel % RING, rows, :], wds.at[to, rows, :], ds_s.at[q, to], ds_r.at[q, to], x_to(step)
        )

    def ways(step, h):
        found = []
        if step < 4 or h == 0:
            found.append((1, -step))
        if step < 4 or h == 1:
            found.append((-1, step))
        return found

    def goes_on(step, h, way):
        return step < 3 or (step == 3 and (h == 0) == (way == 1))

    def z_event(step, h):
        for r in range(Z_PARTS):
            for way, dz in ways(step, h):
                if step > 0:
                    z_copy(dz + way, h, r, way).wait_recv()
                if goes_on(step, h, way):
                    go(z_copy(dz, h, r, way))
        for way, dz in ways(step, h):
            if step > 0 or way == 1:
                go(c_copy(dz, h))

    def x_event(step, h):
        for q in range(h * X_PARTS, (h + 1) * X_PARTS):
            for way, rel in ways(step, h):
                if step > 0:
                    d_copy(rel + way, q, way).wait_recv()
                if goes_on(step, h, way):
                    go(d_copy(rel, q, way))

    row_ids = lax.broadcasted_iota(jnp.int32, (8, 1), 0)
    offs = jnp.zeros((8, 1), jnp.int32)
    for j, off in enumerate(OFFSETS):
        offs = jnp.where(row_ids == j, off, offs)
    locs = l + offs
    locs = jnp.where(locs >= RING, locs - RING, locs)
    targets = jnp.where(row_ids < len(OFFSETS), g * RING + locs, -1).astype(F32)
    slot_ids = lax.broadcasted_iota(jnp.int32, (ROWS, tok_rows), 0).astype(F32)

    OUT = ((1, 4 * ROWS, 0, 4, 2), (7, 3 * ROWS, 2, 2, 2), (6, 0, 4, 6, 1), (2, ROWS, 5, 7, 1))

    def y_copy(p, k):
        off, _, src, dst, n = OUT[k]
        return remote(
            xs.at[p, :, pl.ds(src * width, n * width)], xr.at[p, :, pl.ds(dst * width, n * width)],
            xs_s.at[k, p], xs_r.at[k, p], y_to(off),
        )

    def select(dz):
        p = POS[dz]
        for h in range(2):
            c_copy(dz, h).wait_recv()
        hits = []
        weights = []
        for core in range(2):
            info = xa[p, core, pl.ds(tok_rows, 16), :].astype(F32)
            hit = jnp.zeros((8, tok_rows), F32)
            weight = jnp.zeros((8, tok_rows), F32)
            for k in range(8):
                same = info[k:k + 1, :] == targets
                hit = jnp.where(same, 1.0, hit)
                weight = jnp.where(same, info[8 + k:9 + k, :], weight)
            hits.append(hit)
            weights.append(weight)
        both = jnp.concatenate(hits, axis=0)
        rank = jnp.dot(both.astype(BF16), tri[...], preferred_element_type=F32)
        for core in range(2):
            place = jnp.where(hits[core] > 0.5, rank[8 * core:8 * core + 8, :] + float(core * CAP), -1.0)
            for j in range(len(OFFSETS)):
                same = slot_ids == place[j:j + 1, :]
                where = (p, pl.ds(j * ROWS, ROWS), pl.ds(core * tok_rows, tok_rows))
                sel[where] = jnp.where(same, 1.0, 0.0).astype(BF16)
                selw[where] = jnp.where(same, weights[core][j:j + 1, :], 0.0).astype(BF16)
        first = sel[p, :, pl.ds(0, tok_rows)]
        second = sel[p, :, pl.ds(tok_rows, tok_rows)]
        x0 = (
            jnp.dot(first, xa[p, 0, pl.ds(0, tok_rows), :], preferred_element_type=F32)
            + jnp.dot(second, xa[p, 1, pl.ds(0, tok_rows), :], preferred_element_type=F32)
        ).astype(BF16)
        x1 = (
            jnp.dot(first[2 * ROWS:, :], xb[p, 0], preferred_element_type=F32)
            + jnp.dot(second[2 * ROWS:, :], xb[p, 1], preferred_element_type=F32)
        ).astype(BF16)
        for k, (_, row, src, _, n) in enumerate(OUT):
            xs[p, :, pl.ds(src * width, width)] = x0[row:row + ROWS, :]
            if n == 2:
                xs[p, :, pl.ds((src + 1) * width, width)] = x1[row - 2 * ROWS:row - ROWS, :]
            go(y_copy(p, k))
        xr[p, :, pl.ds(0, width)] = x0[2 * ROWS:3 * ROWS, :]
        xr[p, :, pl.ds(width, width)] = x1[:ROWS, :]

    def gate_up(first, count):
        for p in range(first, first + count):
            for k in range(4):
                y_copy(p, k).wait_recv()
        x = xr[pl.ds(first, count)].reshape(count * ROWS, RING * width)
        rows = pl.ds(first * ROWS, count * ROWS)
        for n in range(ff // 256):
            part = pl.ds(n * 256, 256)
            gate = jnp.dot(x, wgs[:, part], preferred_element_type=F32)
            up = jnp.dot(x, wus[:, part], preferred_element_type=F32)
            hid[rows, part] = (gate / (1.0 + jnp.exp(-gate)) * up).astype(BF16)

    load_d.wait()
    x_event(0, 0)
    x_event(0, 1)
    load_b.wait()
    z_event(0, 1)
    load_i.wait()
    load_g.wait()
    xa[0, c, pl.ds(tok_rows, 16), :] = jnp.concatenate(
        [ids_v[...].astype(F32), gains_v[...].astype(F32)], axis=0
    ).astype(BF16)
    tri[...] = jnp.where(
        lax.broadcasted_iota(jnp.int32, (tok_rows, tok_rows), 0) < lax.broadcasted_iota(jnp.int32, (tok_rows, tok_rows), 1),
        1.0, 0.0,
    ).astype(BF16)
    load_a.wait()
    z_event(0, 0)
    for copy in weight_loads:
        copy.start()
    select(0)
    z_event(1, 1)
    x_event(1, 0)
    z_event(1, 0)
    select(1)
    select(7)
    x_event(1, 1)
    z_event(2, 1)
    z_event(2, 0)
    x_event(2, 0)
    select(2)
    select(6)
    z_event(3, 1)
    for copy in weight_loads:
        copy.wait()
    x_event(2, 1)
    z_event(3, 0)
    gate_up(0, 3)
    select(3)
    select(5)
    z_event(4, 1)
    z_event(4, 0)
    x_event(3, 0)
    select(4)
    gate_up(3, 2)
    x_event(3, 1)
    gate_up(5, 2)

    def b_copy(p, k):
        rel, off, window = BACK[k]
        return remote(ob.at[p, rel], yr.at[p, window], bs.at[k, p], br.at[k, p], y_to(off))

    def down(slot, first, count):
        h = hid[pl.ds(first * ROWS, count * ROWS), :]
        y = jnp.dot(h, wds[slot], preferred_element_type=F32).astype(BF16)
        rel = (t + slot + RING - l) % RING
        for i in range(count):
            ob[first + i, rel] = y[i * ROWS:(i + 1) * ROWS, :]

    def send_back(first, count):
        for p in reversed(range(first, first + count)):
            for k in range(len(BACK)):
                go(b_copy(p, k))

    early = (0, 1, 7, 2, 6, 3, 5)
    for slot in early:
        down(slot, 0, 7)
    gate_up(7, 1)
    for slot in early:
        down(slot, 7, 1)
    x_event(4, 0)
    x_event(4, 1)
    down(4, 5, 3)
    send_back(5, 3)
    down(4, 0, 5)
    send_back(0, 5)

    def p_copy(dz, h):
        p = POS[dz]
        return remote(pk.at[p, other, h], pp.at[p, h], ps.at[p, h], pr.at[p, h], partner)

    def mix(dz):
        p = POS[dz]
        for rel, window in BACK_SELF:
            yr[p, window] = ob[p, rel]
        for k in range(len(BACK)):
            b_copy(p, k).wait_recv()
        for h, row, lo, n in ((1, 2 * ROWS, 5, 3), (0, 0, 0, 5)):
            part = lax.dot_general(
                selw[p, pl.ds(row, n * ROWS), :], yr[p, pl.ds(lo, n)].reshape(n * ROWS, width),
                (((0,), (0,)), ((), ())), preferred_element_type=F32,
            ).astype(BF16)
            pk[p, 0, h] = part[:tok_rows, :]
            pk[p, 1, h] = part[tok_rows:, :]
            go(p_copy(dz, h))

    def rows_of(r):
        return pl.ds(r * piece, piece)

    def chip_sum(dz, h, r):
        p = POS[dz]
        return pk[p, c, h, rows_of(r), :].astype(F32) + pp[p, h, rows_of(r), :].astype(F32)

    def r_copy(way, s, h, r):
        src, dst, send, recv = (sp, rp, rps, rpr) if way == 1 else (sm, rm, rms, rmr)
        return remote(
            src.at[s - 1, h, rows_of(r), :], dst.at[s - 1, h, rows_of(r), :],
            send.at[s - 1, h, r], recv.at[s - 1, h, r], z_to(way),
        )

    def ring(s, h):
        sides = [way for way in (1, -1) if s < 4 or (h == 0) == (way == 1)]
        for way in sides:
            p_copy(s if way == 1 else RING - s, h).wait_recv()
        for r in range(R_PARTS):
            for way in sides:
                value = chip_sum(s if way == 1 else RING - s, h, r)
                if goes_on(s, h, way):
                    r_copy(way, s + 1, h, r).wait_recv()
                    value += (rp if way == 1 else rm)[s, h, rows_of(r), :].astype(F32)
                (sp if way == 1 else sm)[s - 1, h, rows_of(r), :] = value.astype(BF16)
                go(r_copy(way, s, h, r))

    def total(h, r):
        value = chip_sum(0, h, r)
        for way, buf in ((1, rp), (-1, rm)):
            r_copy(way, 1, h, r).wait_recv()
            value += buf[0, h, rows_of(r), :].astype(F32)
        return value

    def way_of(r):
        return y_to(2 if r < R_PARTS // 2 else 6)

    def f_copy(stage, r):
        src, dst = (fs, fa) if stage == 0 else (fa, fr)
        return remote(src.at[rows_of(r), :], dst.at[rows_of(r), :], fsem.at[0, stage, r], fsem.at[1, stage, r], way_of(r))

    mix(4)
    ring(4, 1)
    ring(4, 0)
    mix(3)
    mix(5)
    ring(3, 1)
    ring(3, 0)
    mix(2)
    mix(6)
    ring(2, 1)
    ring(2, 0)
    mix(1)
    mix(7)
    ring(1, 1)
    ring(1, 0)
    mix(0)
    p_copy(0, 1).wait_recv()
    p_copy(0, 0).wait_recv()
    for r in range(R_PARTS):
        fs[rows_of(r), :] = total(1, r).astype(BF16)
        go(f_copy(0, r))
    for r in range(R_PARTS):
        f_copy(0, r).wait_recv()
        go(f_copy(1, r))
    for r in range(R_PARTS):
        own = total(0, r)
        f_copy(1, r).wait_recv()
        o_ref[rows_of(r), :] = (own + fr[rows_of(r), :].astype(F32)).astype(BF16)
    for copy in started:
        copy.wait_send()


def body(tokens, expert_ids, router_weights, w_gate, w_up, w_down):
    rows, width_model = tokens.shape
    ff = w_gate.shape[2]
    width = width_model // RING
    dma = pltpu.SemaphoreType.DMA
    anywhere = pl.BlockSpec(memory_space=pl.ANY)
    return pl.pallas_call(
        kernel,
        out_shape=jax.ShapeDtypeStruct((rows, width), BF16),
        in_specs=[anywhere] * 6,
        out_specs=pl.BlockSpec(memory_space=pltpu.VMEM),
        scratch_shapes=[
            pltpu.VMEM((8, 2, rows + 16, width), BF16),
            pltpu.VMEM((8, 2, rows, width), BF16),
            pltpu.VMEM((8, 5 * ROWS, 2 * rows), BF16),
            pltpu.VMEM((8, 5 * ROWS, 2 * rows), BF16),
            pltpu.VMEM((8, ROWS, 6 * width), BF16),
            pltpu.VMEM((8, ROWS, 8 * width), BF16),
            pltpu.VMEM((width_model, ff), BF16),
            pltpu.VMEM((width_model, ff), BF16),
            pltpu.VMEM((8, ff, width), BF16),
            pltpu.VMEM((8 * ROWS, ff), BF16),
            pltpu.VMEM((8, 8, ROWS, width), BF16),
            pltpu.VMEM((8, 8, ROWS, width), BF16),
            pltpu.VMEM((8, 2, 2, rows, width), BF16),
            pltpu.VMEM((8, 2, rows, width), BF16),
            pltpu.VMEM((4, 2, rows, width), BF16),
            pltpu.VMEM((4, 2, rows, width), BF16),
            pltpu.VMEM((4, 2, rows, width), BF16),
            pltpu.VMEM((4, 2, rows, width), BF16),
            pltpu.VMEM((rows, width), BF16),
            pltpu.VMEM((rows, width), BF16),
            pltpu.VMEM((rows, width), BF16),
            pltpu.VMEM((rows, rows), BF16),
            pltpu.VMEM((8, rows), jnp.int32),
            pltpu.VMEM((8, rows), BF16),
            dma((5,)), dma((2, 8)),
            dma((2, Z_PARTS, 8)), dma((2, Z_PARTS, 8)), dma((2, 8)), dma((2, 8)),
            dma((2 * X_PARTS, 8)), dma((2 * X_PARTS, 8)), dma((4, 8)), dma((4, 8)),
            dma((6, 8)), dma((6, 8)), dma((8, 2)), dma((8, 2)),
            dma((4, 2, R_PARTS)), dma((4, 2, R_PARTS)), dma((4, 2, R_PARTS)), dma((4, 2, R_PARTS)),
            dma((2, 2, R_PARTS)),
        ],
        compiler_params=pltpu.CompilerParams(
            collective_id=0, has_side_effects=True, vmem_limit_bytes=60 * 1024 * 1024
        ),
    )(expert_ids.T, router_weights.T, tokens, w_gate, w_up, w_down)


def solution(mesh):
    placed = (
        P(("grp", "tp"), None),
        P(("grp", "tp"), None),
        P(("grp", "tp"), None),
        P(("grp", "loc"), None, None),
        P(("grp", "loc"), None, None),
        P(("grp", "loc"), None, "tp"),
    )
    return jax.shard_map(
        body, mesh=mesh, in_specs=placed, out_specs=P(("grp", "tp"), "loc"), check_vma=False
    )
```

time: 102 us -> 99.8 us (0.978)
  the two profiles are of different devices: /device:TPU:2 before, /device:TPU:1 now
where the time goes in v2:
time: 99.8 us; the launch traced here: 99.7 us
  Pallas kernels  98.1 us (98%)
  local copies, waits for them, and re-layouts  1.57 us (2%)
    pallas_call x1, Pallas kernels, body(): pl.pallas_call(kernel, out_shape=jax.ShapeDtypeStruct((rows, width), BF16...  98.1 us

profile of v2, /device:TPU:1, one launch (start us, length us, event | category | flops | bytes accessed | tf_op | source)
XLA Modules:
  0.0 99.7 jit_solution(12206177513326526293)
XLA Ops:
  0.0 98.1 %shard_map.64 = bf16[256,256]{1,0:T(8,128)(2,1)} custom-call(s32[8,256]{1,0:T(8,128)} %bitcast.2, bf16[8,256]{1,0:T(8,128)(2,1)} %bitcast.3, bf16[256,2048]{1,0:T(8,128)(2,1)} %tok.1, bf16[1,2048,768]{2,1,0:T(8,128)(2,1)} %wg.1, bf16[1,2048,768]{2,1,0:T(8,128)(2,1)} %wu.1, bf16[1,768,256]{2,1,0:T(8,128)(2,1)} %wd.1), custom_call_target="tpu_custom_call" | custom-call | tf_op jit(solution)/shard_map/pallas_call | solution.py:382
  98.1 1.6 %copy.8 = bf16[256,256]{1,0:T(8,128)(2,1)} copy(bf16[256,256]{1,0:T(8,128)(2,1)} %shard_map.64) | data formatting | bytes 262144
